TPU v7x, 256 devices: a whole 4x4x8 slice. The times are simulated.
256 devices in a mesh: row: 8 (over z), col: 32 (over y, x, core).
Axes of the slice: x: 4, y: 4, z: 8, core: 2. Of those that a mesh axis runs over, the one named last changes fastest.
Arguments:
- factor_tiles: bfloat16 [3, 96, 64, 2048], P(None, 'row', None, 'col'), may hold values from -0.3125 to 0.3125
- tile_row: int32 [3, 96, 32], P(None, 'row', 'col'), may hold values from 0 to 63
- tile_col: int32 [3, 96, 32], P(None, 'row', 'col'), may hold values from 0 to 15
- right_sides: float32 [4, 512, 64, 128], P(None, ('col', 'row')), may hold values from -6 to 6
- diag_inverse: float32 [4, 64, 32768], P(None, None, ('col', 'row')), as said below
Outputs:
- preconditioned: float32 [4, 512, 64, 128], P(None, ('col', 'row'))
Inputs may be any that keep to these rules, and one draw needn't show every extreme that they name: `tile_row`: a block row within its row group. `tile_col`: a block column within its column group. `diag_inverse`: diagonal entries of every block between 0.5 and 2.
All inputs are finite; a program needn't handle non-finite values.
Results may differ from a plain program's by a relative error of at most 0.025.
Values may be sent and summed in bfloat16 or wider, within the bound.
A program may use at most 64 MiB of HBM per device.

v0:
```python
import jax
import jax.numpy as jnp
from jax import lax
from jax.sharding import PartitionSpec as P


def apply_inverse(inverse, vector, transposed):
    matrix = inverse.reshape(inverse.shape[0], -1, inverse.shape[0])
    if transposed:
        return jnp.einsum("cir,irn->icn", matrix, vector, precision=lax.Precision.HIGHEST)
    return jnp.einsum("cir,icn->irn", matrix, vector, precision=lax.Precision.HIGHEST)


def solve_all(factor_tiles, tile_row, tile_col, right_sides, diag_inverse):
    levels = factor_tiles.shape[0]
    rows_dev = right_sides.shape[1]
    group_rows = rows_dev * lax.axis_size("row")
    row_ids = tile_row[:, :, 0]
    col_ids = tile_col[:, :, 0]
    current = apply_inverse(diag_inverse[0], right_sides[0], False)
    solved = [current]
    for section_no in range(1, levels + 1):
        gathered = lax.all_gather(current.astype(jnp.bfloat16), "row", axis=0, tiled=True)
        picked = gathered[col_ids[section_no - 1]]
        products = jnp.einsum(
            "tab,tbn->tan", factor_tiles[section_no - 1], picked, preferred_element_type=jnp.float32
        )
        targets = row_ids[section_no - 1]

        def term(offset, length, products=products, targets=targets):
            places = jnp.arange(length, dtype=jnp.int32)
            select = (targets[:, None] == places[None, :]).astype(jnp.float32)
            return jnp.einsum("tq,tan->qan", select, products, precision=lax.Precision.HIGHEST)

        row_sums = lax.psum_scatter(
            term(jnp.int32(0), lax.axis_size("col") * rows_dev).astype(jnp.bfloat16),
            "col",
            scatter_dimension=0,
            tiled=True,
        ).astype(jnp.float32)
        current = apply_inverse(diag_inverse[section_no], right_sides[section_no] - row_sums, False)
        solved.append(current)
    current = apply_inverse(diag_inverse[levels], solved[levels], True)
    result = [current]
    columns_here = jnp.arange(group_rows, dtype=jnp.int32)
    for section_no in range(levels - 1, -1, -1):
        everyone = lax.all_gather(current.astype(jnp.bfloat16), "col", axis=0, tiled=True)
        picked = everyone[row_ids[section_no]]
        spread = jnp.einsum(
            "tab,tan->tbn", factor_tiles[section_no], picked, preferred_element_type=jnp.float32
        )
        select = (col_ids[section_no][:, None] == columns_here[None, :]).astype(jnp.float32)
        column_sums = jnp.einsum("tj,tbn->jbn", select, spread, precision=lax.Precision.HIGHEST)
        received = lax.psum_scatter(
            column_sums.astype(jnp.bfloat16), "row", scatter_dimension=0, tiled=True
        ).astype(jnp.float32)
        current = apply_inverse(diag_inverse[section_no], solved[section_no] - received, True)
        result.insert(0, current)
    return jnp.stack(result)


def on_device(factor_tiles, tile_row, tile_col, right_sides, diag_inverse):
    return solve_all(factor_tiles, tile_row, tile_col, right_sides, diag_inverse)


def solution(mesh):
    return jax.shard_map(
        on_device,
        mesh=mesh,
        in_specs=(
            P(None, "row", None, "col"),
            P(None, "row", "col"),
            P(None, "row", "col"),
            P(None, ("col", "row"), None, None),
            P(None, None, ("col", "row")),
        ),
        out_specs=P(None, ("col", "row"), None, None),
        check_vma=False,
    )
```

profile of v0, /device:TPU:2, one launch (start us, length us, event | category | flops | bytes accessed | tf_op | source)
XLA Modules:
  0.0 630.8 jit_solution(13500943562827002383)
XLA Ops:
  6.5 0.9 fusion.66
  7.5 1.0 fusion.67
  8.6 28.6 %all_gather.18 = bf16[16,64,128]{2,1,0:T(8,128)(2,1)S(1)} all-gather(bf16[2,64,128]{2,1,0:T(8,128)(2,1)S(1)} %get-tuple-element.21), channel_id=1, replica_groups=mesh['row'=8,'col'=32] {'row'}, dimensions={0}, use_global_device_ids=true | all-gather | bytes 294912 | tf_op jit(solution)/shard_map/all_gather | solution.py:23
  39.3 1.1 convolution_convert_fusion.2
  40.4 1.7 copy.47
  42.3 84.0 %reduce-scatter.7.cloned.1.call-done = bf16[2,64,128]{2,1,0:T(8,128)(2,1)} async-done(((bf16[64,64,128]{2,1,0:T(8,128)(2,1)}), bf16[2,64,128]{2,1,0:T(8,128)(2,1)}) %reduce-scatter.7.cloned.1.call-update) | async-done | bytes 32784 | tf_op jit(solution)/shard_map/reduce_scatter | solution.py:35
  126.3 1.0 fusion.68
  127.3 26.2 %all_gather.19 = bf16[16,64,128]{2,1,0:T(8,128)(2,1)S(1)} all-gather(bf16[2,64,128]{2,1,0:T(8,128)(2,1)S(1)} %get-tuple-element.23), channel_id=1, replica_groups=mesh['row'=8,'col'=32] {'row'}, dimensions={0}, use_global_device_ids=true | all-gather | bytes 294912 | tf_op jit(solution)/shard_map/all_gather | solution.py:23
  154.3 1.1 convolution_convert_fusion.1
  155.4 1.7 copy.50
  157.3 83.2 %reduce-scatter.9.cloned.1.call-done = bf16[2,64,128]{2,1,0:T(8,128)(2,1)} async-done(((bf16[64,64,128]{2,1,0:T(8,128)(2,1)}), bf16[2,64,128]{2,1,0:T(8,128)(2,1)}) %reduce-scatter.9.cloned.1.call-update) | async-done | bytes 32784 | tf_op jit(solution)/shard_map/reduce_scatter | solution.py:35
  240.5 1.0 fusion.69
  241.5 26.3 %all_gather.20 = bf16[16,64,128]{2,1,0:T(8,128)(2,1)S(1)} all-gather(bf16[2,64,128]{2,1,0:T(8,128)(2,1)S(1)} %get-tuple-element.25), channel_id=1, replica_groups=mesh['row'=8,'col'=32] {'row'}, dimensions={0}, use_global_device_ids=true | all-gather | bytes 294912 | tf_op jit(solution)/shard_map/all_gather | solution.py:23
  268.6 1.1 convolution_convert_fusion
  269.7 1.7 copy.53
  271.5 83.2 %reduce-scatter.11.cloned.1.call-done = bf16[2,64,128]{2,1,0:T(8,128)(2,1)} async-done(((bf16[64,64,128]{2,1,0:T(8,128)(2,1)}), bf16[2,64,128]{2,1,0:T(8,128)(2,1)}) %reduce-scatter.11.cloned.1.call-update) | async-done | bytes 32784 | tf_op jit(solution)/shard_map/reduce_scatter | solution.py:35
  354.7 1.0 fusion.21
  355.7 0.8 bitcast_convert_fusion.2
  356.7 48.0 %all-gather.4.cloned.1.call-done = bf16[64,64,128]{2,1,0:T(8,128)(2,1)} async-done(((bf16[2,64,128]{2,1,0:T(8,128)(2,1)}), bf16[64,64,128]{2,1,0:T(8,128)(2,1)}) %all-gather.4.cloned.1.call-update) | async-done | bytes 1048592 | tf_op jit(solution)/shard_map/all_gather | solution.py:47
  404.7 1.8 gather_fusion.3
  407.3 0.8 copy.95
  408.2 36.5 %reduce-scatter.13.cloned.1.call-done = bf16[2,64,128]{2,1,0:T(8,128)(2,1)} async-done(((bf16[16,64,128]{2,1,0:T(8,128)(2,1)}), bf16[2,64,128]{2,1,0:T(8,128)(2,1)}) %reduce-scatter.13.cloned.1.call-update) | async-done | bytes 32784 | tf_op jit(solution)/shard_map/reduce_scatter | solution.py:54
  444.7 1.7 bitcast_convert_fusion.1
  446.4 46.9 %all-gather.6.cloned.1.call-done = bf16[64,64,128]{2,1,0:T(8,128)(2,1)} async-done(((bf16[2,64,128]{2,1,0:T(8,128)(2,1)}), bf16[64,64,128]{2,1,0:T(8,128)(2,1)}) %all-gather.6.cloned.1.call-update) | async-done | bytes 1048592 | tf_op jit(solution)/shard_map/all_gather | solution.py:47
  493.3 1.8 gather_fusion.4
  496.0 0.8 copy.94
  496.8 36.5 %reduce-scatter.15.cloned.1.call-done = bf16[2,64,128]{2,1,0:T(8,128)(2,1)} async-done(((bf16[16,64,128]{2,1,0:T(8,128)(2,1)}), bf16[2,64,128]{2,1,0:T(8,128)(2,1)}) %reduce-scatter.15.cloned.1.call-update) | async-done | bytes 32784 | tf_op jit(solution)/shard_map/reduce_scatter | solution.py:54
  533.4 1.7 bitcast_convert_fusion
  535.1 47.3 %all-gather.8.cloned.1.call-done = bf16[64,64,128]{2,1,0:T(8,128)(2,1)} async-done(((bf16[2,64,128]{2,1,0:T(8,128)(2,1)}), bf16[64,64,128]{2,1,0:T(8,128)(2,1)}) %all-gather.8.cloned.1.call-update) | async-done | bytes 1048592 | tf_op jit(solution)/shard_map/all_gather | solution.py:47
  582.4 1.8 gather_fusion.5
  585.9 36.6 %reduce-scatter.17.cloned.1.call-done = bf16[2,64,128]{2,1,0:T(8,128)(2,1)} async-done(((bf16[16,64,128]{2,1,0:T(8,128)(2,1)}), bf16[2,64,128]{2,1,0:T(8,128)(2,1)}) %reduce-scatter.17.cloned.1.call-update) | async-done | bytes 32784 | tf_op jit(solution)/shard_map/reduce_scatter | solution.py:54
  622.5 1.0 convolution_bitcast_fusion.6
  (54 shorter events, 8.6 us)
Async XLA Ops:
  6.5 32.6 %copy-start = (bf16[3,12,64,64]{3,2,1,0:T(8,128)(2,1)S(1)}, bf16[3,12,64,64]{3,2,1,0:T(8,128)(2,1)}, u32[]{:S(2)}) copy-start(bf16[3,12,64,64]{3,2,1,0:T(8,128)(2,1)} %param.5) | copy-start | bytes 884740
  6.5 119.8 %reduce-scatter.7.cloned.1.call-start = ((), (), s32[]{:S(2)}) async-start(), calls=%async_computation.6 | async-start | bytes 1081344 | tf_op jit(solution)/shard_map/reduce_scatter | solution.py:35
  42.1 84.2 %copy-start.1 = (f32[4,2,64,128]{3,2,1,0:T(8,128)S(1)}, f32[4,2,64,128]{3,2,1,0:T(8,128)}, u32[]{:S(2)}) copy-start(f32[4,2,64,128]{3,2,1,0:T(8,128)} %param.8) | copy-start | bytes 786436
  42.1 198.4 %reduce-scatter.9.cloned.1.call-start = ((), (), s32[]{:S(2)}) async-start(), calls=%async_computation.7 | async-start | bytes 1081344 | tf_op jit(solution)/shard_map/reduce_scatter | solution.py:35
  157.1 197.6 %reduce-scatter.11.cloned.1.call-start = ((), (), s32[]{:S(2)}) async-start(), calls=%async_computation.8 | async-start | bytes 1081344 | tf_op jit(solution)/shard_map/reduce_scatter | solution.py:35
  271.4 85.3 %copy-start.2 = (s32[3,12,1]{1,2,0:T(1,128)S(1)}, s32[3,12,1]{1,2,0:T(1,128)}, u32[]{:S(2)}) copy-start(s32[3,12,1]{1,2,0:T(1,128)} %param.6) | copy-start | bytes 436
  271.4 85.3 %copy-start.3 = (s32[3,12,1]{1,2,0:T(1,128)S(1)}, s32[3,12,1]{1,2,0:T(1,128)}, u32[]{:S(2)}) copy-start(s32[3,12,1]{1,2,0:T(1,128)} %param.7) | copy-start | bytes 436
  271.4 133.3 %all-gather.4.cloned.1.call-start = ((), (), s32[]{:S(2)}) async-start(), calls=%async_computation.9 | async-start | bytes 1081344 | tf_op jit(solution)/shard_map/all_gather | solution.py:47
  356.6 88.1 %reduce-scatter.13.cloned.1.call-start = ((), (), s32[]{:S(2)}) async-start(), calls=%async_computation.10 | async-start | bytes 294912 | tf_op jit(solution)/shard_map/reduce_scatter | solution.py:54
  408.1 85.2 %all-gather.6.cloned.1.call-start = ((), (), s32[]{:S(2)}) async-start(), calls=%async_computation.11 | async-start | bytes 1081344 | tf_op jit(solution)/shard_map/all_gather | solution.py:47
  446.4 87.0 %reduce-scatter.15.cloned.1.call-start = ((), (), s32[]{:S(2)}) async-start(), calls=%async_computation.12 | async-start | bytes 294912 | tf_op jit(solution)/shard_map/reduce_scatter | solution.py:54
  496.8 85.7 %all-gather.8.cloned.1.call-start = ((), (), s32[]{:S(2)}) async-start(), calls=%async_computation.13 | async-start | bytes 1081344 | tf_op jit(solution)/shard_map/all_gather | solution.py:47
  535.0 87.4 %reduce-scatter.17.cloned.1.call-start = ((), (), s32[]{:S(2)}) async-start(), calls=%async_computation.14 | async-start | bytes 294912 | tf_op jit(solution)/shard_map/reduce_scatter | solution.py:54
Sparse Core Ops, SparseCore 0:
  42.2 84.0 reduce-scatter.6
  157.2 83.2 reduce-scatter.8
  271.5 83.1 reduce-scatter.10
  357.4 47.1 all-gather.3
  408.2 36.3 reduce-scatter.12
  447.1 46.1 all-gather.5
  496.9 36.4 reduce-scatter.14
  536.2 46.1 all-gather.7
  586.0 36.3 reduce-scatter.16
where the time goes:
time: 631 us
  waiting for transfers between devices  502 us (80%)
  blocking collectives  81.1 us (13%)
  local copies, waits for them, and re-layouts  16.5 us (3%)
  matrix products  15.6 us (2%)
  between operations  13.5 us (2%)
    reduce_scatter x3, waiting for transfers between devices, solve_all(): lax.psum_scatter(term(jnp.int32(0), lax.axis_size('col') * rows_dev).asty...  250 us
    all_gather x3, waiting for transfers between devices, solve_all(): lax.all_gather(current.astype(jnp.bfloat16), 'col', axis=0, tiled=True)  142 us
    reduce_scatter x3, waiting for transfers between devices, solve_all(): lax.psum_scatter(column_sums.astype(jnp.bfloat16), 'row', scatter_dimensi...  110 us
    all_gather x3, blocking collectives, solve_all(): lax.all_gather(current.astype(jnp.bfloat16), 'row', axis=0, tiled=True)  81.1 us
  transfers between devices with their start and end apart: 9, of which 9 were waited for; matrix products, arithmetic and copies ran while one was open for 0% of the time, Pallas kernels for 0%

commit v1 on v0

--- a/solution.py
+++ b/solution.py
@@ -44,7 +44,12 @@
     result = [current]
     columns_here = jnp.arange(group_rows, dtype=jnp.int32)
     for section_no in range(levels - 1, -1, -1):
-        everyone = lax.all_gather(current.astype(jnp.bfloat16), "col", axis=0, tiled=True)
+        everyone = jnp.concatenate(
+            lax.all_to_all(
+                jnp.stack([current.astype(jnp.bfloat16)] * lax.axis_size("col")), "col", 0, 0
+            ),
+            axis=0,
+        )
         picked = everyone[row_ids[section_no]]
         spread = jnp.einsum(
             "tab,tan->tbn", factor_tiles[section_no], picked, preferred_element_type=jnp.float32

time: 631 us -> 549 us (0.87)
  waiting for transfers between devices: 502 us -> 400 us
  starting transfers between devices: 0.34 us -> 21.1 us
    all_gather x3 -> x0, waiting for transfers between devices: 142 us -> none  [solve_all(): lax.all_gather(current.astype(jnp.bfloat16), 'col', axis=0, tiled=True)]
    all_to_all x0 -> x3, waiting for transfers between devices: none -> 48.1 us  [solve_all(): lax.all_to_all(jnp.stack([current.astype(jnp.bfloat16)] * lax.axis_size('...]
    all_to_all x0 -> x3, starting transfers between devices: none -> 20.9 us  [solve_all(): lax.all_to_all(jnp.stack([current.astype(jnp.bfloat16)] * lax.axis_size('...]
    reduce_scatter x3, waiting for transfers between devices: 110 us -> 101 us  [solve_all(): lax.psum_scatter(column_sums.astype(jnp.bfloat16), 'row', scatter_dimensi...]
where the time goes in v1:
time: 549 us; the launch traced here: 548 us
  waiting for transfers between devices  400 us (73%)
  blocking collectives  81.1 us (15%)
  starting transfers between devices  21.1 us (4%)
  local copies, waits for them, and re-layouts  16.5 us (3%)
  between operations  13.8 us (3%)
  matrix products  13.7 us (2%)
    reduce_scatter x3, waiting for transfers between devices, solve_all(): lax.psum_scatter(term(jnp.int32(0), lax.axis_size('col') * rows_dev).asty...  250 us
    reduce_scatter x3, waiting for transfers between devices, solve_all(): lax.psum_scatter(column_sums.astype(jnp.bfloat16), 'row', scatter_dimensi...  101 us
    all_gather x3, blocking collectives, solve_all(): lax.all_gather(current.astype(jnp.bfloat16), 'row', axis=0, tiled=True)  81.1 us
    all_to_all x3, waiting for transfers between devices, solve_all(): lax.all_to_all(jnp.stack([current.astype(jnp.bfloat16)] * lax.axis_size('...  48.1 us
    all_to_all x3, starting transfers between devices, solve_all(): lax.all_to_all(jnp.stack([current.astype(jnp.bfloat16)] * lax.axis_size('...  20.9 us
  transfers between devices with their start and end apart: 9, of which 9 were waited for; matrix products, arithmetic and copies ran while one was open for 0% of the time, Pallas kernels for 0%

profile of v1, /device:TPU:2, one launch (start us, length us, event | category | flops | bytes accessed | tf_op | source)
XLA Modules:
  0.0 547.8 jit_solution(14052164826490715267)
XLA Ops:
  6.5 0.9 fusion.66
  7.5 1.0 fusion.67
  8.6 28.6 %all_gather.9 = bf16[16,64,128]{2,1,0:T(8,128)(2,1)S(1)} all-gather(bf16[2,64,128]{2,1,0:T(8,128)(2,1)S(1)} %get-tuple-element.21), channel_id=1, replica_groups=mesh['row'=8,'col'=32] {'row'}, dimensions={0}, use_global_device_ids=true | all-gather | bytes 294912 | tf_op jit(solution)/shard_map/all_gather | solution.py:23
  39.3 1.1 convolution_convert_fusion.2
  40.4 1.7 copy.47
  42.3 84.0 %reduce-scatter.7.cloned.1.call-done = bf16[2,64,128]{2,1,0:T(8,128)(2,1)} async-done(((bf16[64,64,128]{2,1,0:T(8,128)(2,1)}), bf16[2,64,128]{2,1,0:T(8,128)(2,1)}) %reduce-scatter.7.cloned.1.call-update) | async-done | bytes 32784 | tf_op jit(solution)/shard_map/reduce_scatter | solution.py:35
  126.3 1.0 fusion.68
  127.3 26.2 %all_gather.10 = bf16[16,64,128]{2,1,0:T(8,128)(2,1)S(1)} all-gather(bf16[2,64,128]{2,1,0:T(8,128)(2,1)S(1)} %get-tuple-element.23), channel_id=1, replica_groups=mesh['row'=8,'col'=32] {'row'}, dimensions={0}, use_global_device_ids=true | all-gather | bytes 294912 | tf_op jit(solution)/shard_map/all_gather | solution.py:23
  154.3 1.1 convolution_convert_fusion.1
  155.4 1.7 copy.50
  157.3 83.2 %reduce-scatter.9.cloned.1.call-done = bf16[2,64,128]{2,1,0:T(8,128)(2,1)} async-done(((bf16[64,64,128]{2,1,0:T(8,128)(2,1)}), bf16[2,64,128]{2,1,0:T(8,128)(2,1)}) %reduce-scatter.9.cloned.1.call-update) | async-done | bytes 32784 | tf_op jit(solution)/shard_map/reduce_scatter | solution.py:35
  240.5 1.0 fusion.69
  241.5 26.3 %all_gather.11 = bf16[16,64,128]{2,1,0:T(8,128)(2,1)S(1)} all-gather(bf16[2,64,128]{2,1,0:T(8,128)(2,1)S(1)} %get-tuple-element.25), channel_id=1, replica_groups=mesh['row'=8,'col'=32] {'row'}, dimensions={0}, use_global_device_ids=true | all-gather | bytes 294912 | tf_op jit(solution)/shard_map/all_gather | solution.py:23
  268.6 1.1 convolution_convert_fusion
  269.7 1.7 copy.53
  271.5 83.2 %reduce-scatter.11.cloned.1.call-done = bf16[2,64,128]{2,1,0:T(8,128)(2,1)} async-done(((bf16[64,64,128]{2,1,0:T(8,128)(2,1)}), bf16[2,64,128]{2,1,0:T(8,128)(2,1)}) %reduce-scatter.11.cloned.1.call-update) | async-done | bytes 32784 | tf_op jit(solution)/shard_map/reduce_scatter | solution.py:35
  354.7 1.0 fusion.21
  356.0 1.2 stack.16
  357.2 6.0 %all-to-all-start = ((bf16[32,2,64,128]{3,2,1,0:T(8,128)(2,1)}), bf16[32,2,64,128]{3,2,1,0:T(8,128)(2,1)S(1)}, u32[]{:S(2)}, u32[]{:S(2)}) async-start(bf16[32,2,64,128]{3,2,1,0:T(8,128)(2,1)} %stack.16), calls=%async_computation.3 | async-start | bytes 2097152 | tf_op jit(solution)/shard_map/all_to_all | solution.py:48
  363.3 16.0 %all-to-all-done = bf16[32,2,64,128]{3,2,1,0:T(8,128)(2,1)S(1)} async-done(((bf16[32,2,64,128]{3,2,1,0:T(8,128)(2,1)}), bf16[32,2,64,128]{3,2,1,0:T(8,128)(2,1)S(1)}, u32[]{:S(2)}, u32[]{:S(2)}) %all-to-all-start) | async-done | bytes 1048608 | tf_op jit(solution)/shard_map/all_to_all | solution.py:48
  381.6 35.6 %reduce-scatter.13.cloned.1.call-done = bf16[2,64,128]{2,1,0:T(8,128)(2,1)} async-done(((bf16[16,64,128]{2,1,0:T(8,128)(2,1)}), bf16[2,64,128]{2,1,0:T(8,128)(2,1)}) %reduce-scatter.13.cloned.1.call-update) | async-done | bytes 32784 | tf_op jit(solution)/shard_map/reduce_scatter | solution.py:59
  417.1 1.0 bitcast_convert_fusion.1
  418.2 1.2 stack.17
  419.4 7.4 %all-to-all-start.1 = ((bf16[32,2,64,128]{3,2,1,0:T(8,128)(2,1)}), bf16[32,2,64,128]{3,2,1,0:T(8,128)(2,1)S(1)}, u32[]{:S(2)}, u32[]{:S(2)}) async-start(bf16[32,2,64,128]{3,2,1,0:T(8,128)(2,1)} %stack.17), calls=%async_computation.5 | async-start | bytes 2097152 | tf_op jit(solution)/shard_map/all_to_all | solution.py:48
  426.9 16.1 %all-to-all-done.1 = bf16[32,2,64,128]{3,2,1,0:T(8,128)(2,1)S(1)} async-done(((bf16[32,2,64,128]{3,2,1,0:T(8,128)(2,1)}), bf16[32,2,64,128]{3,2,1,0:T(8,128)(2,1)S(1)}, u32[]{:S(2)}, u32[]{:S(2)}) %all-to-all-start.1) | async-done | bytes 1048608 | tf_op jit(solution)/shard_map/all_to_all | solution.py:48
  445.2 32.9 %reduce-scatter.15.cloned.1.call-done = bf16[2,64,128]{2,1,0:T(8,128)(2,1)} async-done(((bf16[16,64,128]{2,1,0:T(8,128)(2,1)}), bf16[2,64,128]{2,1,0:T(8,128)(2,1)}) %reduce-scatter.15.cloned.1.call-update) | async-done | bytes 32784 | tf_op jit(solution)/shard_map/reduce_scatter | solution.py:59
  478.1 1.0 bitcast_convert_fusion
  479.2 1.2 stack.18
  480.4 7.4 %all-to-all-start.2 = ((bf16[32,2,64,128]{3,2,1,0:T(8,128)(2,1)}), bf16[32,2,64,128]{3,2,1,0:T(8,128)(2,1)S(1)}, u32[]{:S(2)}, u32[]{:S(2)}) async-start(bf16[32,2,64,128]{3,2,1,0:T(8,128)(2,1)} %stack.18), calls=%async_computation.7 | async-start | bytes 2097152 | tf_op jit(solution)/shard_map/all_to_all | solution.py:48
  487.9 16.1 %all-to-all-done.2 = bf16[32,2,64,128]{3,2,1,0:T(8,128)(2,1)S(1)} async-done(((bf16[32,2,64,128]{3,2,1,0:T(8,128)(2,1)}), bf16[32,2,64,128]{3,2,1,0:T(8,128)(2,1)S(1)}, u32[]{:S(2)}, u32[]{:S(2)}) %all-to-all-start.2) | async-done | bytes 1048608 | tf_op jit(solution)/shard_map/all_to_all | solution.py:48
  506.2 33.0 %reduce-scatter.17.cloned.1.call-done = bf16[2,64,128]{2,1,0:T(8,128)(2,1)} async-done(((bf16[16,64,128]{2,1,0:T(8,128)(2,1)}), bf16[2,64,128]{2,1,0:T(8,128)(2,1)}) %reduce-scatter.17.cloned.1.call-update) | async-done | bytes 32784 | tf_op jit(solution)/shard_map/reduce_scatter | solution.py:59
  539.2 1.0 convolution_bitcast_fusion.6
  (54 shorter events, 12.0 us)
Async XLA Ops:
  6.5 32.6 %copy-start = (bf16[3,12,64,64]{3,2,1,0:T(8,128)(2,1)S(1)}, bf16[3,12,64,64]{3,2,1,0:T(8,128)(2,1)}, u32[]{:S(2)}) copy-start(bf16[3,12,64,64]{3,2,1,0:T(8,128)(2,1)} %param.5) | copy-start | bytes 884740
  6.5 119.8 %reduce-scatter.7.cloned.1.call-start = ((), (), s32[]{:S(2)}) async-start(), calls=%async_computation.9 | async-start | bytes 1081344 | tf_op jit(solution)/shard_map/reduce_scatter | solution.py:35
  42.1 84.2 %copy-start.1 = (f32[4,2,64,128]{3,2,1,0:T(8,128)S(1)}, f32[4,2,64,128]{3,2,1,0:T(8,128)}, u32[]{:S(2)}) copy-start(f32[4,2,64,128]{3,2,1,0:T(8,128)} %param.8) | copy-start | bytes 786436
  42.1 198.4 %reduce-scatter.9.cloned.1.call-start = ((), (), s32[]{:S(2)}) async-start(), calls=%async_computation.10 | async-start | bytes 1081344 | tf_op jit(solution)/shard_map/reduce_scatter | solution.py:35
  157.1 197.6 %reduce-scatter.11.cloned.1.call-start = ((), (), s32[]{:S(2)}) async-start(), calls=%async_computation.11 | async-start | bytes 1081344 | tf_op jit(solution)/shard_map/reduce_scatter | solution.py:35
  357.2 6.0 %copy-start.2 = (s32[3,12,1]{1,2,0:T(1,128)S(1)}, s32[3,12,1]{1,2,0:T(1,128)}, u32[]{:S(2)}) copy-start(s32[3,12,1]{1,2,0:T(1,128)} %param.6) | copy-start | bytes 436
  357.2 6.1 %copy-start.3 = (s32[3,12,1]{1,2,0:T(1,128)S(1)}, s32[3,12,1]{1,2,0:T(1,128)}, u32[]{:S(2)}) copy-start(s32[3,12,1]{1,2,0:T(1,128)} %param.7) | copy-start | bytes 436
  357.2 22.1 %all-to-all-start = ((bf16[32,2,64,128]{3,2,1,0:T(8,128)(2,1)}), bf16[32,2,64,128]{3,2,1,0:T(8,128)(2,1)S(1)}, u32[]{:S(2)}, u32[]{:S(2)}) async-start(bf16[32,2,64,128]{3,2,1,0:T(8,128)(2,1)} %stack.16), calls=%async_computation.3 | async-start | bytes 2097152 | tf_op jit(solution)/shard_map/all_to_all | solution.py:48
  363.2 53.9 %reduce-scatter.13.cloned.1.call-start = ((), (), s32[]{:S(2)}) async-start(), calls=%async_computation.12 | async-start | bytes 294912 | tf_op jit(solution)/shard_map/reduce_scatter | solution.py:59
  419.4 23.5 %all-to-all-start.1 = ((bf16[32,2,64,128]{3,2,1,0:T(8,128)(2,1)}), bf16[32,2,64,128]{3,2,1,0:T(8,128)(2,1)S(1)}, u32[]{:S(2)}, u32[]{:S(2)}) async-start(bf16[32,2,64,128]{3,2,1,0:T(8,128)(2,1)} %stack.17), calls=%async_computation.5 | async-start | bytes 2097152 | tf_op jit(solution)/shard_map/all_to_all | solution.py:48
  426.8 51.3 %reduce-scatter.15.cloned.1.call-start = ((), (), s32[]{:S(2)}) async-start(), calls=%async_computation.13 | async-start | bytes 294912 | tf_op jit(solution)/shard_map/reduce_scatter | solution.py:59
  480.4 23.6 %all-to-all-start.2 = ((bf16[32,2,64,128]{3,2,1,0:T(8,128)(2,1)}), bf16[32,2,64,128]{3,2,1,0:T(8,128)(2,1)S(1)}, u32[]{:S(2)}, u32[]{:S(2)}) async-start(bf16[32,2,64,128]{3,2,1,0:T(8,128)(2,1)} %stack.18), calls=%async_computation.7 | async-start | bytes 2097152 | tf_op jit(solution)/shard_map/all_to_all | solution.py:48
  487.9 51.3 %reduce-scatter.17.cloned.1.call-start = ((), (), s32[]{:S(2)}) async-start(), calls=%async_computation.14 | async-start | bytes 294912 | tf_op jit(solution)/shard_map/reduce_scatter | solution.py:59
Sparse Core Ops, SparseCore 0:
  42.2 84.0 reduce-scatter.6
  157.2 83.2 reduce-scatter.8
  271.5 83.1 reduce-scatter.10
  381.7 35.3 reduce-scatter.12
  445.3 32.7 reduce-scatter.14
  506.3 32.7 reduce-scatter.16
